TPU v7x, 128 devices: a whole 4x4x4 slice. The times are simulated.
128 devices in a mesh: dp: 16 (over z, x), tensor: 8 (over y, core).
Axes of the slice: x: 4, y: 4, z: 4, core: 2. Of those that a mesh axis runs over, the one named last changes fastest.
Arguments:
- tokens: bfloat16 [128, 128, 8192], P('dp', None, 'tensor'), may hold values from -6 to 6
- shared_prefix_tokens: bfloat16 [16, 256, 8192], P('dp', None, 'tensor'), may hold values from -6 to 6
- input_norm_gain: bfloat16 [8192], replicated, may hold values from 0.5 to 8
- query_weight: bfloat16 [8192, 8192], P(None, 'tensor'), may hold values from -0.0625 to 0.0625
- key_weight: bfloat16 [8192, 1024], P(None, 'tensor'), may hold values from -0.0625 to 0.0625
- value_weight: bfloat16 [8192, 1024], P(None, 'tensor'), may hold values from -0.0625 to 0.0625
- adapter_down_weight: bfloat16 [64, 8192, 16], P('dp', 'tensor'), may hold values from -0.0625 to 0.0625
- adapter_up_weight: bfloat16 [64, 16, 8192], P('dp', None, 'tensor'), may hold values from -0.75 to 0.75
- adapter_position: int32 [64], replicated, may hold values from 0 to 63, as said below
- request_adapter: int32 [128], P('dp'), may hold values from 0 to 63, as said below
- request_group: int32 [128], P('dp'), may hold values from 0 to 15
- lengths: int32 [128], P('dp'), may hold values from 1 to 128
- request_page_table: int32 [128, 1], P('dp'), may hold values from 0 to 127, as said below
Outputs:
- context: bfloat16 [128, 128, 8192], P('dp', None, 'tensor')
- paged_key_values: bfloat16 [128, 2, 128, 1024], P('dp', None, None, 'tensor')
Inputs may be any that keep to these rules, and one draw needn't show every extreme that they name: A permutation: adapter a is held at slot adapter_position[a], on index adapter_position[a] // 4 of dp. `request_adapter`: the 8 requests of one index of dp use adapters held by 8 different indices of dp. `request_page_table`: the requests of index i of dp use the pages i * 8 to (i + 1) * 8 - 1, each page once.
All inputs are finite; a program needn't handle non-finite values.
Results may differ from a plain program's by a relative error of at most 0.011.
The roundings to bfloat16 on the way count: a program that leaves them out, or rounds other values in their place, can miss the bound.
Values may be sent and summed in bfloat16 or wider, within the bound.
No kernel may reach another device: no remote copies, remote signals or barrier semaphores. Data moves between devices by JAX's collectives and lax.ppermute only.
A program may use at most 128 MiB of HBM per device.

v0:
```python
import jax
import jax.numpy as jnp
from jax import lax
from jax.sharding import PartitionSpec as P

HEAD_WIDTH = 128
ADAPTER_RANK = 16
PAGE_TOKENS = 128
EPS = 1e-05
THETA = 500000.0
ADAPTER_SCALE = 2.0


def rope_tables(positions, width):
    half = width // 2
    freq = THETA ** (-(jnp.arange(half, dtype=jnp.float32) * 2.0 / width))
    angle = positions.astype(jnp.float32)[:, None] * freq[None, :]
    return (jnp.cos(angle), jnp.sin(angle))


def apply_rope(values, cosine, sine):
    half = values.shape[-1] // 2
    first = values[..., :half]
    second = values[..., half:]
    cos_b = cosine[:, None, :]
    sin_b = sine[:, None, :]
    return jnp.concatenate(
        [first * cos_b - second * sin_b, second * cos_b + first * sin_b], axis=-1
    )


def normalize(rows, gain):
    values = rows.astype(jnp.float32)
    scale = lax.rsqrt(jnp.mean(values * values, axis=-1, keepdims=True) + EPS)
    return (values * scale * gain.astype(jnp.float32)).astype(jnp.bfloat16)


def on_device(
    tokens,
    shared_prefix_tokens,
    input_norm_gain,
    query_weight,
    key_weight,
    value_weight,
    adapter_down_weight,
    adapter_up_weight,
    adapter_position,
    request_adapter,
    request_group,
    lengths,
    request_page_table,
):
    req_dev, seq_len, d_part = tokens.shape
    grp_dev, pre_len, _ = shared_prefix_tokens.shape
    q_width = query_weight.shape[1]
    kv_width = key_weight.shape[1]
    q_heads = q_width // HEAD_WIDTH
    kv_local = kv_width // HEAD_WIDTH
    group_members = q_heads // kv_local
    token_rows = req_dev * seq_len
    column = lax.axis_index("tensor")
    place = lax.axis_index("dp")
    full_tokens, full_prefix = (
        lax.all_gather(tokens.reshape(token_rows, d_part), "tensor", axis=1, tiled=True),
        lax.all_gather(
            shared_prefix_tokens.reshape(grp_dev * pre_len, d_part), "tensor", axis=1, tiled=True
        ),
    )
    normed_input = normalize(full_tokens, input_norm_gain)
    prefix_normed = normalize(full_prefix, input_norm_gain)
    pre_cos, pre_sin = rope_tables(jnp.arange(pre_len), HEAD_WIDTH)
    pre_keys = jnp.dot(prefix_normed, key_weight, preferred_element_type=jnp.float32).reshape(
        grp_dev, pre_len, kv_local, HEAD_WIDTH
    )
    pre_keys = (
        apply_rope(pre_keys, pre_cos, pre_sin)
        .astype(jnp.bfloat16)
        .reshape(grp_dev, pre_len, kv_width)
    )
    pre_vals = (
        jnp.dot(prefix_normed, value_weight, preferred_element_type=jnp.float32)
        .astype(jnp.bfloat16)
        .reshape(grp_dev, pre_len, kv_width)
    )
    all_pairs = lax.all_gather(jnp.stack([pre_keys, pre_vals], 1), "dp", axis=0, tiled=True)
    table_ids = jnp.arange(adapter_position.shape[0])
    slots = jnp.sum(
        jnp.where(request_adapter[:, None] == table_ids[None, :], adapter_position[None, :], 0),
        axis=1,
    )
    local_rows = lax.dynamic_slice_in_dim(normed_input, column * d_part, d_part, 1)
    row_slot = jnp.repeat(slots, seq_len)
    page_piece = lax.all_gather(adapter_down_weight, "dp", axis=0, tiled=True)
    count = page_piece.shape[0]
    part = jnp.einsum("td,ndr->tnr", local_rows, page_piece, preferred_element_type=jnp.float32)
    pick = row_slot[:, None] == jnp.arange(count)[None, :]
    partial_low = jnp.sum(jnp.where(pick[:, :, None], part, 0.0), axis=1)
    low_rank_rows = lax.psum(partial_low, "tensor").astype(jnp.bfloat16)
    page_piece = lax.all_gather(adapter_up_weight, "dp", axis=0, tiled=True)
    count = page_piece.shape[0]
    pick = (row_slot[:, None] == jnp.arange(count)[None, :]).astype(jnp.bfloat16)
    spread = (pick[:, :, None] * low_rank_rows[:, None, :]).reshape(
        token_rows, count * ADAPTER_RANK
    )
    summed_rows = jnp.dot(
        spread,
        page_piece.reshape(count * ADAPTER_RANK, q_width),
        preferred_element_type=jnp.float32,
    )
    adapter_term = (ADAPTER_SCALE * summed_rows).astype(jnp.bfloat16)
    own_cos, own_sin = rope_tables(pre_len + jnp.arange(seq_len), HEAD_WIDTH)
    query_rows = jnp.dot(
        normed_input, query_weight, preferred_element_type=jnp.float32
    ) + adapter_term.astype(jnp.float32)
    query_rows = apply_rope(
        query_rows.reshape(req_dev, seq_len, q_heads, HEAD_WIDTH), own_cos, own_sin
    ).astype(jnp.bfloat16)
    key_rows = jnp.dot(normed_input, key_weight, preferred_element_type=jnp.float32).reshape(
        req_dev, seq_len, kv_local, HEAD_WIDTH
    )
    key_rows = apply_rope(key_rows, own_cos, own_sin).astype(jnp.bfloat16)
    value_rows = (
        jnp.dot(normed_input, value_weight, preferred_element_type=jnp.float32)
        .astype(jnp.bfloat16)
        .reshape(req_dev, seq_len, kv_local, HEAD_WIDTH)
    )
    live = jnp.arange(seq_len)[None, :] < lengths[:, None]
    key_rows = jnp.where(live[:, :, None, None], key_rows, jnp.zeros_like(key_rows))
    value_rows = jnp.where(live[:, :, None, None], value_rows, jnp.zeros_like(value_rows))
    chosen = all_pairs[request_group]
    all_keys = jnp.concatenate(
        [chosen[:, 0].reshape(req_dev, pre_len, kv_local, HEAD_WIDTH), key_rows], 1
    )
    all_vals = jnp.concatenate(
        [chosen[:, 1].reshape(req_dev, pre_len, kv_local, HEAD_WIDTH), value_rows], 1
    )
    grouped_query = query_rows.reshape(req_dev, seq_len, kv_local, group_members, HEAD_WIDTH)
    scores = jnp.einsum(
        "btkgd,bskd->bkgts", grouped_query, all_keys, preferred_element_type=jnp.float32
    ) * HEAD_WIDTH ** (-0.5)
    seen = jnp.arange(pre_len + seq_len)[None, :]
    allowed = (seen < pre_len) | (seen - pre_len <= jnp.arange(seq_len)[:, None])
    scores = jnp.where(allowed[None, None, None], scores, -1e30)
    top = jnp.max(scores, axis=-1, keepdims=True)
    weights = jnp.exp(scores - top)
    probs = (weights / jnp.sum(weights, axis=-1, keepdims=True)).astype(jnp.bfloat16)
    attention_output = jnp.einsum(
        "bkgts,bskd->btkgd", probs, all_vals, preferred_element_type=jnp.float32
    )
    attention_output = jnp.where(live[:, :, None, None, None], attention_output, 0.0)
    context = attention_output.reshape(req_dev, seq_len, q_width).astype(jnp.bfloat16)
    pages_req = seq_len // PAGE_TOKENS
    page_blocks = jnp.stack(
        [
            key_rows.reshape(req_dev, pages_req, PAGE_TOKENS, kv_width),
            value_rows.reshape(req_dev, pages_req, PAGE_TOKENS, kv_width),
        ],
        2,
    )
    page_blocks = page_blocks.reshape(req_dev * pages_req, 2, PAGE_TOKENS, kv_width)
    local_page = request_page_table.reshape(-1) - place * (req_dev * pages_req)
    paged_key_values = jnp.zeros_like(page_blocks).at[local_page].set(page_blocks)
    return (context, paged_key_values)


def solution(mesh):
    in_specs = (
        P("dp", None, "tensor"),
        P("dp", None, "tensor"),
        P(),
        P(None, "tensor"),
        P(None, "tensor"),
        P(None, "tensor"),
        P("dp", "tensor", None),
        P("dp", None, "tensor"),
        P(),
        P("dp"),
        P("dp"),
        P("dp"),
        P("dp", None),
    )
    out_specs = (P("dp", None, "tensor"), P("dp", None, None, "tensor"))
    return jax.shard_map(
        on_device, mesh=mesh, in_specs=in_specs, out_specs=out_specs, check_vma=False
    )
```

profile of v0, /device:TPU:0, one launch (start us, length us, event | category | flops | bytes accessed | tf_op | source)
XLA Modules:
  0.0 344.5 jit_solution(120121396503228455)
XLA Ops:
  7.2 0.0 copy-start
  7.2 0.0 all-gather.15.cloned.1.call-start
  7.2 0.7 all-gather.15.cloned.1.call-update
  7.9 0.0 all-gather.7.cloned.1.call-start
  8.0 0.7 convert_element_type.114
  8.7 35.6 %all-gather.15.cloned.1.call-done = bf16[1,256,8192]{2,1,0:T(8,128)(2,1)} async-done(((bf16[1,256,1024]{2,1,0:T(8,128)(2,1)}), bf16[1,256,8192]{2,1,0:T(8,128)(2,1)}) %all-gather.15.cloned.1.call-update) | async-done | bytes 4194320 | tf_op jit(solution)/shard_map/all_gather | solution.py:65
  44.3 3.3 fusion.5
  47.6 0.2 copy-done.4
  47.8 3.3 fusion.33
  51.1 0.3 fusion.58
  51.5 0.0 copy-start.13
  51.5 0.0 copy-start.14
  51.5 1.7 fusion.39
  53.3 0.8 copy.63
  54.1 0.0 all-gather.7.cloned.1.call-update
  54.1 0.0 all-gather.9.cloned.1.call-start
  54.1 0.7 all-gather.9.cloned.1.call-update
  54.8 0.0 all-gather.11.cloned.1.call-start
  54.9 0.5 all-gather.11.cloned.1.call-update
  55.4 0.0 all-gather.13.cloned.1.call-start
  55.4 0.5 all-gather.13.cloned.1.call-update
  56.0 0.2 select_reduce_fusion.1
  56.2 0.1 broadcast_bitcast_fusion
  56.3 0.1 fusion.65
  56.4 0.3 multiply_cosine_fusion
  56.7 0.6 iota_compare_fusion.3
  57.3 0.6 pad_clamp_fusion
  57.9 0.2 fusion.48
  58.1 0.5 fusion.59
  58.6 40.8 %all-gather.7.cloned.1.call-done = bf16[16,2,256,128]{3,2,1,0:T(8,128)(2,1)} async-done(((bf16[1,2,256,128]{3,2,1,0:T(8,128)(2,1)}), bf16[16,2,256,128]{3,2,1,0:T(8,128)(2,1)}) %all-gather.7.cloned.1.call-update) | async-done | bytes 2097168 | tf_op jit(solution)/shard_map/all_gather | solution.py:85
  99.4 2.5 gather_fusion
  101.9 1.0 fusion.67
  102.9 2.0 copy.78
  105.0 80.4 %all-gather.9.cloned.1.call-done = bf16[1024,8192]{1,0:T(8,128)(2,1)} async-done(((bf16[1024,1024]{1,0:T(8,128)(2,1)}), bf16[1024,8192]{1,0:T(8,128)(2,1)}) %all-gather.9.cloned.1.call-update) | async-done | bytes 16777232 | tf_op jit(solution)/shard_map/all_gather | solution.py:64
  185.4 7.5 %fusion = f32[1024]{0:T(1024)S(1)} fusion(bf16[1024,8192]{1,0:T(8,128)(2,1)} %all-gather.9.cloned.1.call-done), kind=kLoop, calls=%fused_computation.4 | loop fusion | flops 25164800 | bytes 16781312 | tf_op jit(solution)/shard_map/reduce_sum | solution.py:34
  192.9 3.2 copy-done.2
  196.0 8.3 %fusion.2 = bf16[1024,8192]{1,0:T(8,128)(2,1)} fusion(bf16[1024,8192]{1,0:T(8,128)(2,1)S(1)} %copy-done.2, f32[8192]{0:T(1024)S(1)} %convert_element_type.114, f32[1024]{0:T(1024)S(1)} %add_rsqrt_fusion), kind=kLoop, calls=%fused_computation.6 | loop fusion | flops 33554432 | bytes 33591296 | tf_op jit(solution)/shard_map/convert_element_type | solution.py:35
  204.3 29.0 %all-gather.11.cloned.1.call-done = bf16[64,1024,16]{1,2,0:T(8,128)(2,1)} async-done(((bf16[4,1024,16]{1,2,0:T(8,128)(2,1)}), bf16[64,1024,16]{1,2,0:T(8,128)(2,1)}) %all-gather.11.cloned.1.call-update) | async-done | bytes 2097168 | tf_op jit(solution)/shard_map/all_gather | solution.py:93
  233.3 5.1 %select_reduce_fusion = f32[1024,16]{0,1:T(8,128)S(1)} fusion(pred[1024,64]{0,1:T(8,128)(4,1)S(1)} %get-tuple-element.23, bf16[64,1024,16]{1,2,0:T(8,128)(2,1)} %all-gather.11.cloned.1.call-done, bf16[1024,8192]{1,0:T(8,128)(2,1)} %fusion.2, s32[]{:T(128)S(6)} %select_n.72), kind=kOutput, calls=%fused_computation.27 | convolution fusion | flops 2149564416 | bytes 4325380 | tf_op jit(solution)/shard_map/td,ndr->tnr/dot_general | solution.py:95
  238.4 25.3 %psum.7 = bf16[1024,16]{0,1:T(8,128)(2,1)S(1)} all-reduce(f32[1024,16]{0,1:T(8,128)S(1)} %select_reduce_fusion), channel_id=1, replica_groups=mesh['dp'=16,'tensor'=8] {'tensor'}, use_global_device_ids=true, to_apply=%region_4.5 | all-reduce | flops 16384 | bytes 98304 | tf_op jit(solution)/shard_map/psum | solution.py:98
  263.7 8.5 %convolution_convert_fusion = bf16[1024,128]{1,0:T(8,128)(2,1)S(1)} fusion(bf16[1024,8192]{1,0:T(8,128)(2,1)} %fusion.2, bf16[8192,128]{1,0:T(8,128)(2,1)S(1)} %copy-done), kind=kOutput, calls=%fused_computation.38 | convolution fusion | flops 2147614720 | bytes 19136512 | tf_op jit(solution)/shard_map/dot_general | solution.py:123
  272.2 2.4 copy-done.3
  274.6 0.6 copy-done.11
  275.2 4.5 %fusion.68 = f32[1024,128]{1,0:T(8,128)S(1)} fusion(bf16[1024,8192]{1,0:T(8,128)(2,1)S(1)} %copy-done.3, bf16[8192,128]{1,0:T(8,128)(2,1)S(1)} %copy-done.11), kind=kOutput, calls=%fused_computation.101 | convolution fusion | flops 2147483648 | bytes 19398656 | tf_op jit(solution)/shard_map/dot_general | solution.py:118
  279.7 0.1 all-gather.13.cloned.1.call-done
  279.8 5.4 %fusion.12 = bf16[1024,1024]{1,0:T(8,128)(2,1)S(1)} fusion(bf16[64,16,1024]{2,1,0:T(8,128)(2,1)} %all-gather.13.cloned.1.call-done, bf16[1024,16]{0,1:T(8,128)(2,1)S(1)} %psum.7, bf16[1024,64]{0,1:T(8,128)(2,1)S(1)} %get-tuple-element.22), kind=kOutput, calls=%fused_computation.23 | convolution fusion | flops 2150629376 | bytes 4358144 | tf_op jit(solution)/shard_map/dot_general | solution.py:105
  285.3 22.6 %add_bitcast_fusion = f32[128,8,8,128]{3,1,2,0:T(8,128)S(1)} fusion(bf16[1024,1024]{1,0:T(8,128)(2,1)S(1)} %fusion.12, bf16[1024,8192]{1,0:T(8,128)(2,1)} %fusion.2, bf16[8192,1024]{1,0:T(8,128)(2,1)} %param.16), kind=kOutput, calls=%fused_computation.26 | convolution fusion | flops 17181966336 | bytes 39845888 | tf_op jit(solution)/shard_map/dot_general | solution.py:112
  307.9 1.0 copy.82
  308.9 4.6 %fusion.66 = (f32[8,128,8,64]{3,2,1,0:T(8,128)}, f32[8,128,8,64]{3,2,1,0:T(8,128)}) fusion(f32[8,128,8,128]{3,2,1,0:T(8,128)S(1)} %bitcast.99), kind=kLoop, calls=%fused_computation.99 | loop fusion | bytes 8388608 | tf_op jit(solution)/shard_map/slice | solution.py:23
  313.4 0.2 subtract_convert_fusion.1
  313.7 0.3 broadcast_select_fusion.1
  314.0 0.8 copy.65
  314.9 5.2 %subtract_convert_fusion = (bf16[8,128,8,64]{3,1,2,0:T(8,128)(2,1)S(1)}, bf16[8,128,8,64]{3,1,2,0:T(8,128)(2,1)S(1)}) fusion(f32[8,128,8,64]{3,2,1,0:T(8,128)} %get-tuple-element.15, f32[8,128,8,64]{3,2,1,0:T(8,128)} %get-tuple-element.14, f32[128,64]{1,0:T(8,128)S(1)} %get-tuple-element.29, f32[128,64]{1,0:T(8,128)S(1)} %get-tuple-element.28), kind=kLoop, calls=%fused_computation.25 | loop fusion | flops 4194304 | bytes 6356992 | tf_op jit(solution)/shard_map/convert.4
  320.1 3.1 fusion.4
  323.2 0.0 copy-start.8
  323.2 3.2 fusion.3
  326.5 5.3 %fusion.11 = bf16[8,1,128,8,128]{4,2,3,0,1:T(8,128)(2,1)} fusion(f32[8,8,128]{2,1,0:T(8,128)S(1)} %fusion.3, f32[8,8,128]{2,1,0:T(8,128)S(1)} %get-tuple-element.30, f32[8,384,128,8]{2,1,3,0:T(8,128)S(1)} %get-tuple-element.31, pred[128,384]{0,1:T(8,128)(4,1)S(1)} %fusion.48, pred[8,128]{1,0:T(8,128)(4,1)S(1)} %copy-done.9, ...), kind=kOutput, calls=%fused_computation.21 | convolution fusion | flops 824705024 | bytes 15582208 | tf_op jit(solution)/shard_map/bkgts,bskd->btkgd/dot_general | solution.py:147
  331.7 4.1 %copy.73 = bf16[8,128,1024]{2,1,0:T(8,128)(2,1)} copy(bf16[8,128,1024]{1,2,0:T(8,128)(2,1)} %bitcast.103) | data formatting | bytes 4194304
  335.8 0.3 maximum_select_fusion.1
  336.1 0.1 maximum_bitcast_fusion.4
  336.2 0.1 broadcast_in_dim.108
  336.3 0.9 scatter_fusion
  337.2 0.0 copy-start.6
  337.2 0.8 copy-done.6
  (34 shorter events, 0.1 us)
Async XLA Ops:
  7.2 44.3 %copy-start = (bf16[8192,128]{1,0:T(8,128)(2,1)S(1)}, bf16[8192,128]{1,0:T(8,128)(2,1)}, u32[]{:S(2)}) copy-start(bf16[8192,128]{1,0:T(8,128)(2,1)} %param.18) | copy-start | bytes 6291460
  7.2 37.2 %all-gather.15.cloned.1.call-start = ((), (), s32[]{:S(2)}) async-start(), calls=%async_computation.4 | async-start | bytes 4718592 | tf_op jit(solution)/shard_map/all_gather | solution.py:65
  7.9 91.5 %all-gather.7.cloned.1.call-start = ((), (), s32[]{:S(2)}) async-start(), calls=%async_computation | async-start | bytes 2228224 | tf_op jit(solution)/shard_map/all_gather | solution.py:85
  44.3 3.4 %copy-start.4 = (bf16[1,256,8192]{2,1,0:T(8,128)(2,1)S(1)}, bf16[1,256,8192]{2,1,0:T(8,128)(2,1)}, u32[]{:S(2)}) copy-start(bf16[1,256,8192]{2,1,0:T(8,128)(2,1)} %all-gather.15.cloned.1.call-done) | copy-start | bytes 12582916
  51.5 4.6 %copy-start.12 = (s32[64]{0:T(128)S(1)}, s32[64]{0:T(128)}, u32[]{:S(2)}) copy-start(s32[64]{0:T(128)} %param.21) | copy-start | bytes 772
  51.5 4.6 %copy-start.13 = (s32[8]{0:T(128)S(1)}, s32[8]{0:T(128)}, u32[]{:S(2)}) copy-start(s32[8]{0:T(128)} %param.22) | copy-start | bytes 100
  51.5 5.2 %copy-start.14 = (s32[8]{0:T(128)S(1)}, s32[8]{0:T(128)}, u32[]{:S(2)}) copy-start(s32[8]{0:T(128)} %param.24) | copy-start | bytes 100
  51.5 5.8 %copy-start.15 = (s32[8]{0:T(128)S(1)}, s32[8]{0:T(128)}, u32[]{:S(2)}) copy-start(s32[8]{0:T(128)} %param.23) | copy-start | bytes 100
  51.5 6.6 %copy-start.16 = (s32[8,1]{0,1:T(1,128)S(1)}, s32[8,1]{0,1:T(1,128)}, u32[]{:S(2)}) copy-start(s32[8,1]{0,1:T(1,128)} %param.25) | copy-start | bytes 100
  54.1 131.3 %all-gather.9.cloned.1.call-start = ((), (), s32[]{:S(2)}) async-start(), calls=%async_computation.1 | async-start | bytes 18874368 | tf_op jit(solution)/shard_map/all_gather | solution.py:64
  54.8 178.5 %all-gather.11.cloned.1.call-start = ((), (), s32[]{:S(2)}) async-start(), calls=%async_computation.2 | async-start | bytes 2228224 | tf_op jit(solution)/shard_map/all_gather | solution.py:93
  55.4 224.4 %all-gather.13.cloned.1.call-start = ((), (), s32[]{:S(2)}) async-start(), calls=%async_computation.3 | async-start | bytes 2228224 | tf_op jit(solution)/shard_map/all_gather | solution.py:99
  185.4 10.7 %copy-start.2 = (bf16[1024,8192]{1,0:T(8,128)(2,1)S(1)}, bf16[1024,8192]{1,0:T(8,128)(2,1)}, u32[]{:S(2)}) copy-start(bf16[1024,8192]{1,0:T(8,128)(2,1)} %all-gather.9.cloned.1.call-done) | copy-start | bytes 50331652
  263.7 10.9 %copy-start.3 = (bf16[1024,8192]{1,0:T(8,128)(2,1)S(1)}, bf16[1024,8192]{1,0:T(8,128)(2,1)}, u32[]{:S(2)}) copy-start(bf16[1024,8192]{1,0:T(8,128)(2,1)} %fusion.2) | copy-start | bytes 50331652
  263.7 11.5 %copy-start.11 = (bf16[8192,128]{1,0:T(8,128)(2,1)S(1)}, bf16[8192,128]{1,0:T(8,128)(2,1)}, u32[]{:S(2)}) copy-start(bf16[8192,128]{1,0:T(8,128)(2,1)} %param.17) | copy-start | bytes 6291460
  308.9 4.8 %copy-start.9 = (pred[8,128]{1,0:T(8,128)(4,1)S(1)}, pred[8,128]{1,0:T(8,128)(4,1)}, u32[]{:S(2)}) copy-start(pred[8,128]{1,0:T(8,128)(4,1)} %iota_compare_fusion.3) | copy-start | bytes 3076
  314.9 5.2 %copy-start.5 = (bf16[8,256,1,128]{3,1,0,2:T(8,128)(2,1)S(1)}, bf16[8,256,1,128]{3,1,0,2:T(8,128)(2,1)}, u32[]{:S(2)}) copy-start(bf16[8,256,1,128]{3,1,0,2:T(8,128)(2,1)} %get-tuple-element.17) | copy-start | bytes 1572868
  323.2 3.2 copy-start.7
  323.2 3.2 copy-start.8
  331.7 4.6 %copy-start.10 = (s32[8]{0:T(128)S(1)}, s32[8]{0:T(128)}, u32[]{:S(2)}) copy-start(s32[8]{0:T(128)} %fusion.59) | copy-start | bytes 100
  331.7 6.2 %copy-start.1 = (bf16[8192,128]{1,0:T(8,128)(2,1)S(1)}, bf16[8192,128]{1,0:T(8,128)(2,1)}, u32[]{:S(2)}) copy-start(bf16[8192,128]{1,0:T(8,128)(2,1)} %param.18) | copy-start | bytes 6291460
  337.2 0.8 copy-start.6
Sparse Core Ops, SparseCore 0:
  9.7 34.5 all-gather.14
  54.2 45.1 all-gather.6
  101.1 84.1 all-gather.8
  187.4 45.8 all-gather.10
  235.3 44.5 all-gather.12
where the time goes:
time: 345 us
  waiting for transfers between devices  188 us (54%)
  matrix products  59.5 us (17%)
  other arithmetic  31.9 us (9%)
  blocking collectives  25.3 us (7%)
  local copies, waits for them, and re-layouts  25.1 us (7%)
  between operations  14.2 us (4%)
    all_gather x1, waiting for transfers between devices, on_device(): lax.all_gather(tokens.reshape(token_rows, d_part), 'tensor', axis=1, tile...  80.4 us
    all_gather x1, waiting for transfers between devices, on_device(): lax.all_gather(jnp.stack([pre_keys, pre_vals], 1), 'dp', axis=0, tiled=True)  40.8 us
    all_gather x1, waiting for transfers between devices, on_device(): lax.all_gather(shared_prefix_tokens.reshape(grp_dev * pre_len, d_part), '...  35.6 us
    all_gather x1, waiting for transfers between devices, on_device(): page_piece = lax.all_gather(adapter_down_weight, 'dp', axis=0, tiled=True)  29 us
    psum x1, blocking collectives, on_device(): low_rank_rows = lax.psum(partial_low, 'tensor').astype(jnp.bfloat16)  25.3 us
    dot_general x1, matrix products, on_device(): jnp.dot(normed_input, query_weight, preferred_element_type=jnp.float32)  22.6 us
    unnamed x37, local copies, waits for them, and re-layouts  14.3 us
    reduce_sum x2, other arithmetic, normalize(): scale = lax.rsqrt(jnp.mean(values * values, axis=-1, keepdims=True) + EPS)  10.7 us
  transfers between devices with their start and end apart: 5, of which 5 were waited for; matrix products, arithmetic and copies ran while one was open for 12% of the time, Pallas kernels for 0%

commit v1 on v0

--- a/solution.py
+++ b/solution.py
@@ -82,7 +82,9 @@
         .astype(jnp.bfloat16)
         .reshape(grp_dev, pre_len, kv_width)
     )
-    all_pairs = lax.all_gather(jnp.stack([pre_keys, pre_vals], 1), "dp", axis=0, tiled=True)
+    x = jnp.stack([pre_keys, pre_vals], 1)
+    copies = jnp.concatenate([x] * lax.axis_size("dp"), axis=0)
+    all_pairs = lax.all_to_all(copies, "dp", 0, 0, tiled=True)
     table_ids = jnp.arange(adapter_position.shape[0])
     slots = jnp.sum(
         jnp.where(request_adapter[:, None] == table_ids[None, :], adapter_position[None, :], 0),

time: 345 us -> 291 us (0.84)
  waiting for transfers between devices: 188 us -> 126 us
  starting transfers between devices: 0.19 us -> 7.15 us
    all_gather x1, waiting for transfers between devices: 80.4 us -> 29.4 us  [on_device(): lax.all_gather(tokens.reshape(token_rows, d_part), 'tensor', axis=1, tile...]
    all_gather x1 -> x0, waiting for transfers between devices: 40.8 us -> none  [on_device(): lax.all_gather(jnp.stack([pre_keys, pre_vals], 1), 'dp', axis=0, tiled=True)]
    all_to_all x0 -> x1, waiting for transfers between devices: none -> 30.9 us  [on_device(): all_pairs = lax.all_to_all(copies, 'dp', 0, 0, tiled=True)]
    all_to_all x0 -> x1, starting transfers between devices: none -> 7 us  [on_device(): all_pairs = lax.all_to_all(copies, 'dp', 0, 0, tiled=True)]
  transfers between devices with their start and end apart: 5 -> 5, of which waited for: 5 -> 5; matrix products, arithmetic and copies ran while one was open for 12% -> 18% of each run, Pallas kernels for 0% -> 0%
where the time goes in v1:
time: 291 us; the launch traced here: 290 us
  waiting for transfers between devices  126 us (43%)
  matrix products  59.6 us (20%)
  other arithmetic  31.8 us (11%)
  local copies, waits for them, and re-layouts  26.5 us (9%)
  blocking collectives  25.3 us (9%)
  between operations  14.1 us (5%)
  starting transfers between devices  7.15 us (2%)
    all_gather x1, waiting for transfers between devices, on_device(): lax.all_gather(shared_prefix_tokens.reshape(grp_dev * pre_len, d_part), '...  33.6 us
    all_to_all x1, waiting for transfers between devices, on_device(): all_pairs = lax.all_to_all(copies, 'dp', 0, 0, tiled=True)  30.9 us
    all_gather x1, waiting for transfers between devices, on_device(): lax.all_gather(tokens.reshape(token_rows, d_part), 'tensor', axis=1, tile...  29.4 us
    all_gather x1, waiting for transfers between devices, on_device(): page_piece = lax.all_gather(adapter_down_weight, 'dp', axis=0, tiled=True)  29.1 us
    psum x1, blocking collectives, on_device(): low_rank_rows = lax.psum(partial_low, 'tensor').astype(jnp.bfloat16)  25.3 us
    dot_general x1, matrix products, on_device(): jnp.dot(normed_input, query_weight, preferred_element_type=jnp.float32)  22.6 us
    unnamed x37, local copies, waits for them, and re-layouts  14.4 us
    reduce_sum x2, other arithmetic, normalize(): scale = lax.rsqrt(jnp.mean(values * values, axis=-1, keepdims=True) + EPS)  10.7 us
  transfers between devices with their start and end apart: 5, of which 5 were waited for; matrix products, arithmetic and copies ran while one was open for 18% of the time, Pallas kernels for 0%

profile of v1, /device:TPU:0, one launch (start us, length us, event | category | flops | bytes accessed | tf_op | source)
XLA Modules:
  0.0 290.2 jit_solution(1514906805974163235)
XLA Ops:
  7.2 0.0 copy-start
  7.2 0.0 all-gather.12.cloned.1.call-start
  7.2 0.7 all-gather.12.cloned.1.call-update
  7.9 0.0 all-gather.6.cloned.1.call-start
  8.0 0.7 all-gather.6.cloned.1.call-update
  8.7 0.0 all-gather.8.cloned.1.call-start
  8.7 0.7 all-gather.8.cloned.1.call-update
  9.4 0.0 all-gather.10.cloned.1.call-start
  9.4 0.5 all-gather.10.cloned.1.call-update
  10.0 0.7 convert_element_type.114
  10.7 33.6 %all-gather.12.cloned.1.call-done = bf16[1,256,8192]{2,1,0:T(8,128)(2,1)} async-done(((bf16[1,256,1024]{2,1,0:T(8,128)(2,1)}), bf16[1,256,8192]{2,1,0:T(8,128)(2,1)}) %all-gather.12.cloned.1.call-update) | async-done | bytes 4194320 | tf_op jit(solution)/shard_map/all_gather | solution.py:65
  44.3 3.3 %fusion.5 = f32[256]{0:T(256)S(1)} fusion(bf16[1,256,8192]{2,1,0:T(8,128)(2,1)} %all-gather.12.cloned.1.call-done), kind=kLoop, calls=%fused_computation.14 | loop fusion | flops 6291200 | bytes 4195328 | tf_op jit(solution)/shard_map/reduce_sum | solution.py:34
  47.6 0.2 copy-done.4
  47.8 3.3 %fusion.33 = f32[1,256,1,128]{1,3,2,0:T(8,128)S(1)} fusion(bf16[8192,128]{1,0:T(8,128)(2,1)} %param.17, bf16[1,256,8192]{2,1,0:T(8,128)(2,1)S(1)} %copy-done.4, f32[8192]{0:T(1024)S(1)} %convert_element_type.114, f32[256]{0:T(256)S(1)} %add_rsqrt_fusion.1), kind=kOutput, calls=%fused_computation.41 | convolution fusion | flops 545259520 | bytes 6456320 | tf_op jit(solution)/shard_map/dot_general | solution.py:72
  51.1 0.3 fusion.58
  51.5 1.7 fusion.39
  53.2 0.0 copy-start.12
  53.2 0.0 copy-start.13
  53.2 0.0 copy-start.14
  53.3 0.1 copy.49
  53.4 1.8 concatenate.61
  55.2 7.0 %all-to-all-start = ((bf16[16,2,256,128]{3,2,1,0:T(8,128)(2,1)}), bf16[16,2,256,128]{3,2,1,0:T(8,128)(2,1)}, u32[]{:S(2)}, u32[]{:S(2)}) async-start(bf16[16,2,256,128]{3,2,1,0:T(8,128)(2,1)} %concatenate.61), calls=%async_computation | async-start | bytes 4194304 | tf_op jit(solution)/shard_map/all_to_all | solution.py:87
  62.3 0.6 pad_clamp_fusion
  62.9 0.2 select_reduce_fusion.1
  63.1 0.5 fusion.59
  63.6 0.7 iota_compare_fusion.3
  64.2 0.1 broadcast_bitcast_fusion
  64.3 0.2 fusion.48
  64.5 0.3 multiply_cosine_fusion
  64.8 0.1 fusion.65
  64.8 30.9 %all-to-all-done = bf16[16,2,256,128]{3,2,1,0:T(8,128)(2,1)} async-done(((bf16[16,2,256,128]{3,2,1,0:T(8,128)(2,1)}), bf16[16,2,256,128]{3,2,1,0:T(8,128)(2,1)}, u32[]{:S(2)}, u32[]{:S(2)}) %all-to-all-start) | async-done | bytes 2097184 | tf_op jit(solution)/shard_map/all_to_all | solution.py:87
  95.7 2.7 gather_fusion
  98.4 1.0 fusion.67
  99.4 2.1 copy.64
  101.5 29.4 %all-gather.6.cloned.1.call-done = bf16[1024,8192]{1,0:T(8,128)(2,1)} async-done(((bf16[1024,1024]{1,0:T(8,128)(2,1)}), bf16[1024,8192]{1,0:T(8,128)(2,1)}) %all-gather.6.cloned.1.call-update) | async-done | bytes 16777232 | tf_op jit(solution)/shard_map/all_gather | solution.py:64
  130.9 7.5 %fusion = f32[1024]{0:T(1024)S(1)} fusion(bf16[1024,8192]{1,0:T(8,128)(2,1)} %all-gather.6.cloned.1.call-done), kind=kLoop, calls=%fused_computation.4 | loop fusion | flops 25164800 | bytes 16781312 | tf_op jit(solution)/shard_map/reduce_sum | solution.py:34
  138.4 3.2 %copy-done.2 = bf16[1024,8192]{1,0:T(8,128)(2,1)S(1)} copy-done((bf16[1024,8192]{1,0:T(8,128)(2,1)S(1)}, bf16[1024,8192]{1,0:T(8,128)(2,1)}, u32[]{:S(2)}) %copy-start.2) | copy-done | bytes 16777240
  141.6 8.3 %fusion.2 = bf16[1024,8192]{1,0:T(8,128)(2,1)} fusion(bf16[1024,8192]{1,0:T(8,128)(2,1)S(1)} %copy-done.2, f32[8192]{0:T(1024)S(1)} %convert_element_type.114, f32[1024]{0:T(1024)S(1)} %add_rsqrt_fusion), kind=kLoop, calls=%fused_computation.6 | loop fusion | flops 33554432 | bytes 33591296 | tf_op jit(solution)/shard_map/convert_element_type | solution.py:35
  149.9 29.1 %all-gather.8.cloned.1.call-done = bf16[64,1024,16]{1,2,0:T(8,128)(2,1)} async-done(((bf16[4,1024,16]{1,2,0:T(8,128)(2,1)}), bf16[64,1024,16]{1,2,0:T(8,128)(2,1)}) %all-gather.8.cloned.1.call-update) | async-done | bytes 2097168 | tf_op jit(solution)/shard_map/all_gather | solution.py:95
  179.0 5.1 %select_reduce_fusion = f32[1024,16]{0,1:T(8,128)S(1)} fusion(pred[1024,64]{0,1:T(8,128)(4,1)S(1)} %get-tuple-element.21, bf16[64,1024,16]{1,2,0:T(8,128)(2,1)} %all-gather.8.cloned.1.call-done, bf16[1024,8192]{1,0:T(8,128)(2,1)} %fusion.2, s32[]{:T(128)S(6)} %select_n.72), kind=kOutput, calls=%fused_computation.27 | convolution fusion | flops 2149564416 | bytes 4325380 | tf_op jit(solution)/shard_map/td,ndr->tnr/dot_general | solution.py:97
  184.1 25.3 %psum.7 = bf16[1024,16]{0,1:T(8,128)(2,1)S(1)} all-reduce(f32[1024,16]{0,1:T(8,128)S(1)} %select_reduce_fusion), channel_id=1, replica_groups=mesh['dp'=16,'tensor'=8] {'tensor'}, use_global_device_ids=true, to_apply=%region_4.5 | all-reduce | flops 16384 | bytes 98304 | tf_op jit(solution)/shard_map/psum | solution.py:100
  209.4 8.5 %convolution_convert_fusion = bf16[1024,128]{1,0:T(8,128)(2,1)S(1)} fusion(bf16[1024,8192]{1,0:T(8,128)(2,1)} %fusion.2, bf16[8192,128]{1,0:T(8,128)(2,1)S(1)} %copy-done), kind=kOutput, calls=%fused_computation.38 | convolution fusion | flops 2147614720 | bytes 19136512 | tf_op jit(solution)/shard_map/dot_general | solution.py:125
  217.9 2.4 copy-done.3
  220.3 0.6 copy-done.11
  220.9 4.5 %fusion.68 = f32[1024,128]{1,0:T(8,128)S(1)} fusion(bf16[1024,8192]{1,0:T(8,128)(2,1)S(1)} %copy-done.3, bf16[8192,128]{1,0:T(8,128)(2,1)S(1)} %copy-done.11), kind=kOutput, calls=%fused_computation.101 | convolution fusion | flops 2147483648 | bytes 19398656 | tf_op jit(solution)/shard_map/dot_general | solution.py:120
  225.4 0.1 all-gather.10.cloned.1.call-done
  225.6 5.5 %fusion.12 = bf16[1024,1024]{1,0:T(8,128)(2,1)S(1)} fusion(bf16[64,16,1024]{2,1,0:T(8,128)(2,1)} %all-gather.10.cloned.1.call-done, bf16[1024,16]{0,1:T(8,128)(2,1)S(1)} %psum.7, bf16[1024,64]{0,1:T(8,128)(2,1)S(1)} %get-tuple-element.20), kind=kOutput, calls=%fused_computation.23 | convolution fusion | flops 2150629376 | bytes 4358144 | tf_op jit(solution)/shard_map/dot_general | solution.py:107
  231.0 22.6 %add_bitcast_fusion = f32[128,8,8,128]{3,1,2,0:T(8,128)S(1)} fusion(bf16[1024,1024]{1,0:T(8,128)(2,1)S(1)} %fusion.12, bf16[1024,8192]{1,0:T(8,128)(2,1)} %fusion.2, bf16[8192,1024]{1,0:T(8,128)(2,1)} %param.16), kind=kOutput, calls=%fused_computation.26 | convolution fusion | flops 17181966336 | bytes 39845888 | tf_op jit(solution)/shard_map/dot_general | solution.py:114
  253.6 1.0 copy.68
  254.6 4.5 %fusion.66 = (f32[8,128,8,64]{3,2,1,0:T(8,128)}, f32[8,128,8,64]{3,2,1,0:T(8,128)}) fusion(f32[8,128,8,128]{3,2,1,0:T(8,128)S(1)} %bitcast.101), kind=kLoop, calls=%fused_computation.99 | loop fusion | bytes 8388608 | tf_op jit(solution)/shard_map/slice | solution.py:23
  259.2 0.2 subtract_convert_fusion.1
  259.4 0.3 broadcast_select_fusion.1
  259.7 0.8 copy.51
  260.6 5.2 %subtract_convert_fusion = (bf16[8,128,8,64]{3,1,2,0:T(8,128)(2,1)S(1)}, bf16[8,128,8,64]{3,1,2,0:T(8,128)(2,1)S(1)}) fusion(f32[8,128,8,64]{3,2,1,0:T(8,128)} %get-tuple-element.13, f32[8,128,8,64]{3,2,1,0:T(8,128)} %get-tuple-element.12, f32[128,64]{1,0:T(8,128)S(1)} %get-tuple-element.27, f32[128,64]{1,0:T(8,128)S(1)} %get-tuple-element.26), kind=kLoop, calls=%fused_computation.25 | loop fusion | flops 4194304 | bytes 6356992 | tf_op jit(solution)/shard_map/convert.4
  265.8 3.1 %fusion.4 = (f32[8,8,128]{2,1,0:T(8,128)S(1)}, f32[8,384,128,8]{2,1,3,0:T(8,128)S(1)}) fusion(pred[128,384]{0,1:T(8,128)(4,1)S(1)} %fusion.48, bf16[8,128,8,64]{3,1,2,0:T(8,128)(2,1)S(1)} %get-tuple-element.11, bf16[8,128,8,64]{3,1,2,0:T(8,128)(2,1)S(1)} %get-tuple-element.10, bf16[8,128,1,128]{3,1,0,2:T(8,128)(2,1)S(1)} %get-tuple-element.25, ...), kind=kOutput, calls=%fused_computation.13 | convolution fusion | flops 820502528 | bytes 15548416 | tf_op jit(solution)/shard_map/btkgd,bskd->bkgts/dot_general | solution.py:140
  269.0 0.0 copy-start.8
  269.0 3.2 %fusion.3 = f32[8,8,128]{2,1,0:T(8,128)S(1)} fusion(f32[8,384,128,8]{2,1,3,0:T(8,128)S(1)} %get-tuple-element.29, f32[8,8,128]{2,1,0:T(8,128)S(1)} %get-tuple-element.28, pred[128,384]{0,1:T(8,128)(4,1)S(1)} %fusion.48), kind=kLoop, calls=%fused_computation.10 | loop fusion | flops 12574720 | bytes 12697600 | tf_op jit(solution)/shard_map/reduce_sum | solution.py:148
  272.2 5.3 %fusion.11 = bf16[8,1,128,8,128]{4,2,3,0,1:T(8,128)(2,1)} fusion(f32[8,8,128]{2,1,0:T(8,128)S(1)} %fusion.3, f32[8,8,128]{2,1,0:T(8,128)S(1)} %get-tuple-element.28, f32[8,384,128,8]{2,1,3,0:T(8,128)S(1)} %get-tuple-element.29, pred[128,384]{0,1:T(8,128)(4,1)S(1)} %fusion.48, pred[8,128]{1,0:T(8,128)(4,1)S(1)} %copy-done.9, ...), kind=kOutput, calls=%fused_computation.21 | convolution fusion | flops 824705024 | bytes 15582208 | tf_op jit(solution)/shard_map/bkgts,bskd->btkgd/dot_general | solution.py:149
  277.5 4.1 %copy.59 = bf16[8,128,1024]{2,1,0:T(8,128)(2,1)} copy(bf16[8,128,1024]{1,2,0:T(8,128)(2,1)} %bitcast.105) | data formatting | bytes 4194304
  281.5 0.3 maximum_select_fusion.1
  281.8 0.1 maximum_bitcast_fusion.4
  281.9 0.1 broadcast_in_dim.108
  282.1 0.9 scatter_fusion
  282.9 0.8 copy-done.6
  (34 shorter events, 0.2 us)
Async XLA Ops:
  7.2 44.3 %copy-start = (bf16[8192,128]{1,0:T(8,128)(2,1)S(1)}, bf16[8192,128]{1,0:T(8,128)(2,1)}, u32[]{:S(2)}) copy-start(bf16[8192,128]{1,0:T(8,128)(2,1)} %param.18) | copy-start | bytes 6291460
  7.2 37.2 %all-gather.12.cloned.1.call-start = ((), (), s32[]{:S(2)}) async-start(), calls=%async_computation.4 | async-start | bytes 4718592 | tf_op jit(solution)/shard_map/all_gather | solution.py:65
  7.9 123.0 %all-gather.6.cloned.1.call-start = ((), (), s32[]{:S(2)}) async-start(), calls=%async_computation.1 | async-start | bytes 18874368 | tf_op jit(solution)/shard_map/all_gather | solution.py:64
  8.7 170.3 %all-gather.8.cloned.1.call-start = ((), (), s32[]{:S(2)}) async-start(), calls=%async_computation.2 | async-start | bytes 2228224 | tf_op jit(solution)/shard_map/all_gather | solution.py:95
  9.4 216.2 %all-gather.10.cloned.1.call-start = ((), (), s32[]{:S(2)}) async-start(), calls=%async_computation.3 | async-start | bytes 2228224 | tf_op jit(solution)/shard_map/all_gather | solution.py:101
  44.3 3.4 %copy-start.4 = (bf16[1,256,8192]{2,1,0:T(8,128)(2,1)S(1)}, bf16[1,256,8192]{2,1,0:T(8,128)(2,1)}, u32[]{:S(2)}) copy-start(bf16[1,256,8192]{2,1,0:T(8,128)(2,1)} %all-gather.12.cloned.1.call-done) | copy-start | bytes 12582916
  53.2 9.0 %copy-start.12 = (s32[8]{0:T(128)S(1)}, s32[8]{0:T(128)}, u32[]{:S(2)}) copy-start(s32[8]{0:T(128)} %param.23) | copy-start | bytes 100
  53.2 9.6 %copy-start.13 = (s32[64]{0:T(128)S(1)}, s32[64]{0:T(128)}, u32[]{:S(2)}) copy-start(s32[64]{0:T(128)} %param.21) | copy-start | bytes 772
  53.2 9.6 %copy-start.14 = (s32[8]{0:T(128)S(1)}, s32[8]{0:T(128)}, u32[]{:S(2)}) copy-start(s32[8]{0:T(128)} %param.22) | copy-start | bytes 100
  53.2 9.8 %copy-start.15 = (s32[8,1]{0,1:T(1,128)S(1)}, s32[8,1]{0,1:T(1,128)}, u32[]{:S(2)}) copy-start(s32[8,1]{0,1:T(1,128)} %param.25) | copy-start | bytes 100
  53.3 10.3 %copy-start.16 = (s32[8]{0:T(128)S(1)}, s32[8]{0:T(128)}, u32[]{:S(2)}) copy-start(s32[8]{0:T(128)} %param.24) | copy-start | bytes 100
  55.2 40.5 %all-to-all-start = ((bf16[16,2,256,128]{3,2,1,0:T(8,128)(2,1)}), bf16[16,2,256,128]{3,2,1,0:T(8,128)(2,1)}, u32[]{:S(2)}, u32[]{:S(2)}) async-start(bf16[16,2,256,128]{3,2,1,0:T(8,128)(2,1)} %concatenate.61), calls=%async_computation | async-start | bytes 4194304 | tf_op jit(solution)/shard_map/all_to_all | solution.py:87
  130.9 10.7 %copy-start.2 = (bf16[1024,8192]{1,0:T(8,128)(2,1)S(1)}, bf16[1024,8192]{1,0:T(8,128)(2,1)}, u32[]{:S(2)}) copy-start(bf16[1024,8192]{1,0:T(8,128)(2,1)} %all-gather.6.cloned.1.call-done) | copy-start | bytes 50331652
  209.4 10.9 %copy-start.3 = (bf16[1024,8192]{1,0:T(8,128)(2,1)S(1)}, bf16[1024,8192]{1,0:T(8,128)(2,1)}, u32[]{:S(2)}) copy-start(bf16[1024,8192]{1,0:T(8,128)(2,1)} %fusion.2) | copy-start | bytes 50331652
  209.4 11.5 %copy-start.11 = (bf16[8192,128]{1,0:T(8,128)(2,1)S(1)}, bf16[8192,128]{1,0:T(8,128)(2,1)}, u32[]{:S(2)}) copy-start(bf16[8192,128]{1,0:T(8,128)(2,1)} %param.17) | copy-start | bytes 6291460
  254.6 4.8 %copy-start.9 = (pred[8,128]{1,0:T(8,128)(4,1)S(1)}, pred[8,128]{1,0:T(8,128)(4,1)}, u32[]{:S(2)}) copy-start(pred[8,128]{1,0:T(8,128)(4,1)} %iota_compare_fusion.3) | copy-start | bytes 3076
  260.6 5.2 %copy-start.5 = (bf16[8,256,1,128]{3,1,0,2:T(8,128)(2,1)S(1)}, bf16[8,256,1,128]{3,1,0,2:T(8,128)(2,1)}, u32[]{:S(2)}) copy-start(bf16[8,256,1,128]{3,1,0,2:T(8,128)(2,1)} %get-tuple-element.15) | copy-start | bytes 1572868
  268.9 3.2 %copy-start.7 = (bf16[8,1,256,128]{2,3,0,1:T(8,128)(2,1)S(1)}, bf16[8,1,256,128]{2,3,0,1:T(8,128)(2,1)}, u32[]{:S(2)}) copy-start(bf16[8,1,256,128]{2,3,0,1:T(8,128)(2,1)} %copy.64) | copy-start | bytes 1572868
  269.0 3.2 %copy-start.8 = (bf16[8,128,1,128]{1,3,0,2:T(8,128)(2,1)S(1)}, bf16[8,128,1,128]{1,3,0,2:T(8,128)(2,1)}, u32[]{:S(2)}) copy-start(bf16[8,128,1,128]{1,3,0,2:T(8,128)(2,1)} %copy.51) | copy-start | bytes 786436
  277.5 4.6 %copy-start.10 = (s32[8]{0:T(128)S(1)}, s32[8]{0:T(128)}, u32[]{:S(2)}) copy-start(s32[8]{0:T(128)} %fusion.59) | copy-start | bytes 100
  277.5 6.2 %copy-start.1 = (bf16[8192,128]{1,0:T(8,128)(2,1)S(1)}, bf16[8192,128]{1,0:T(8,128)(2,1)}, u32[]{:S(2)}) copy-start(bf16[8192,128]{1,0:T(8,128)(2,1)} %param.18) | copy-start | bytes 6291460
  282.9 0.8 copy-start.6
Sparse Core Ops, SparseCore 0:
  9.7 34.5 all-gather.11
  46.0 84.8 all-gather.5
  133.1 45.8 all-gather.7
  181.0 44.5 all-gather.9
